TPU v7x, 32 devices: a whole 2x2x4 slice. The times are simulated.
32 devices in a mesh: dp: 2 (over core), tok: 4 (over y, x), exp: 4 (over z).
Axes of the slice: x: 2, y: 2, z: 4, core: 2. Of those that a mesh axis runs over, the one named last changes fastest.
Arguments:
- tokens: bfloat16 [16, 1024, 1280], P(('dp', 'exp'), 'tok'), parts along dimension 0, may hold values from -64 to 64
- router: bfloat16 [1280, 64], P(None, 'dp'), parts along dimension 1, may hold values from -1 to 1
- image_counts: int32 [16, 16], P(('dp', 'exp')), parts along dimension 0, may hold values from 1 to 64, as said below
- image_offsets: int32 [16, 16], P(('dp', 'exp')), parts along dimension 0, may hold values from 0 to 960, as said below
- expert_in: bfloat16 [32, 1280, 4096], P('exp', None, 'tok'), may hold values from -0.15625 to 0.15625
- expert_out: bfloat16 [32, 4096, 1280], P('exp', 'tok'), may hold values from -0.09375 to 0.09375
Outputs:
- moe_out: bfloat16 [16, 1024, 1280], P(('dp', 'exp'), 'tok'), parts along dimension 0
There are 2 independent parts, one for each index of `dp`. A program takes and returns all parts, laid end to end along the dimension named above; an argument that names none is the same for every part. Nothing has to cross between parts.
Inputs may be any that keep to these rules, and one draw needn't show every extreme that they name: Each image of a sequence covers image_counts positions from its image_offsets; the images of one sequence are disjoint, in order of rising offsets, and lie inside the sequence of 1024 positions; the last image of every sequence has 1024 // 16 positions. `image_offsets`: offsets rise along each sequence; the last image of every sequence ends at the sequence's end.
All inputs are finite; a program needn't handle non-finite values.
Results may differ from a plain program's by a relative error of at most 0.012.
Values may be sent and summed in bfloat16 or wider, within the bound.
No kernel may reach another device: no remote copies, remote signals or barrier semaphores. Data moves between devices by JAX's collectives and lax.ppermute only.
A program may use at most 128 MiB of HBM per device.

v0:
```python
import jax
import jax.numpy as jnp
from jax import lax
from jax.sharding import PartitionSpec as P


def combined_all(part, axis, combine):
    gathered = jax.tree.map(lambda a: lax.all_gather(a, axis), part)

    def take(source):
        return jax.tree.map(lambda a: lax.dynamic_index_in_dim(a, source, 0, False), gathered)

    return lax.fori_loop(
        1, lax.axis_size(axis), lambda source, state: combine(state, take(source)), take(0)
    )


def merge_parts(earlier, later_part):
    top_value = jnp.maximum(earlier[0], later_part[0])
    first_scale = jnp.exp(earlier[0] - top_value)
    second_scale = jnp.exp(later_part[0] - top_value)
    totals = earlier[1] * first_scale + later_part[1] * second_scale
    slot_sums = earlier[2] * first_scale[..., None] + later_part[2] * second_scale[..., None]
    return (top_value, totals, slot_sums)


def shards(tokens, router, image_counts, image_offsets, expert_in, expert_out):
    block_len = tokens.shape[1]
    where_at = lax.axis_index("tok") * block_len + jnp.arange(block_len, dtype=jnp.int32)
    image_ends = image_offsets + image_counts
    inside = (where_at[None, :, None] >= image_offsets[:, None, :]) & (
        where_at[None, :, None] < image_ends[:, None, :]
    )
    live_mask = jnp.any(inside, axis=-1)
    logits = jnp.einsum("bnd,ds->bns", tokens, router, preferred_element_type=jnp.float32)
    local_peak = jnp.max(jnp.where(live_mask[..., None], logits, -1e30), axis=1)
    weights = jnp.where(live_mask[..., None], jnp.exp(logits - local_peak[:, None, :]), 0.0)
    totals = jnp.sum(weights, axis=1)
    slot_sums = jnp.einsum(
        "bns,bnd->bsd", weights.astype(jnp.bfloat16), tokens, preferred_element_type=jnp.float32
    )
    totals, slot_sums = (totals, slot_sums)
    column_peak, totals, slot_sums = combined_all(
        (local_peak, totals, slot_sums), "tok", merge_parts
    )
    slot_in = (slot_sums / totals[..., None]).astype(jnp.bfloat16)
    owned_slots = lax.all_to_all(slot_in, "exp", split_axis=1, concat_axis=0, tiled=True)
    hidden = jax.nn.gelu(
        jnp.einsum("bed,edf->bef", owned_slots, expert_in, preferred_element_type=jnp.float32),
        approximate=False,
    ).astype(jnp.bfloat16)
    partial_out = jnp.einsum("bef,efd->bed", hidden, expert_out, preferred_element_type=jnp.float32)
    summed = lax.psum(partial_out, "tok")
    slot_out = lax.all_to_all(
        summed.astype(jnp.bfloat16), "exp", split_axis=0, concat_axis=1, tiled=True
    )
    combine_weights = jax.nn.softmax(logits, axis=-1).astype(jnp.bfloat16)
    mixed_out = jnp.einsum(
        "bns,bsd->bnd", combine_weights, slot_out, preferred_element_type=jnp.float32
    )
    return jnp.where(live_mask[..., None], mixed_out, 0.0).astype(jnp.bfloat16)


def solution(mesh):
    placed = (
        P(("dp", "exp"), "tok", None),
        P(None, "dp"),
        P(("dp", "exp"), None),
        P(("dp", "exp"), None),
        P("exp", None, "tok"),
        P("exp", "tok", None),
    )
    return jax.shard_map(
        shards, mesh=mesh, in_specs=placed, out_specs=P(("dp", "exp"), "tok", None), check_vma=False
    )
```

profile of v0, /device:TPU:0, one launch (start us, length us, event | category | flops | bytes accessed | tf_op | source)
XLA Modules:
  0.0 114.1 jit_solution(2261706719610102142)
XLA Ops:
  6.5 0.0 copy-start
  6.5 0.0 all-gather.7.cloned.1.call-start
  6.5 0.8 add.77
  7.3 0.8 and_reduce_fusion
  8.1 0.0 copy-done
  8.1 1.5 %select_reduce_fusion = (f32[2,32]{1,0:T(2,128)S(1)}, f32[2,256,32]{1,2,0:T(8,128)S(1)}) fusion(pred[2,256]{1,0:T(4,128)(4,1)S(1)} %and_reduce_fusion, bf16[2,256,1280]{2,1,0:T(8,128)(2,1)S(1)} %copy-done, bf16[1280,32]{0,1:T(8,128)(2,1)} %param.9), kind=kOutput, calls=%fused_computation.76 | convolution fusion | flops 41975744 | bytes 1458944 | tf_op jit(solution)/shard_map/bnd,ds->bns/dot_general | solution.py:35
  9.6 1.1 fusion.62
  10.7 0.0 all-gather.7.cloned.1.call-update
  10.7 0.2 fusion.61
  10.9 9.6 %all-gather.4 = f32[4,2,32]{2,1,0:T(2,128)S(1)} all-gather(f32[1,2,32]{2,1,0:T(2,128)S(1)} %bitcast.130), channel_id=3, replica_groups=mesh['dp'=2,'tok'=4,'exp'=4] {'tok'}, dimensions={0}, use_global_device_ids=true | all-gather | bytes 1280 | tf_op jit(solution)/shard_map/all_gather | solution.py:8
  20.5 8.1 %all-gather.3 = f32[4,2,32]{2,1,0:T(2,128)S(1)} all-gather(f32[1,2,32]{2,1,0:T(2,128)S(1)} %bitcast.129), channel_id=2, replica_groups=mesh['dp'=2,'tok'=4,'exp'=4] {'tok'}, dimensions={0}, use_global_device_ids=true | all-gather | bytes 1280 | tf_op jit(solution)/shard_map/all_gather | solution.py:8
  28.5 13.8 %all-gather.7.cloned.1.call-done = f32[8,32,1280]{2,1,0:T(8,128)} async-done(((f32[2,32,1280]{2,1,0:T(8,128)}), f32[8,32,1280]{2,1,0:T(8,128)}) %all-gather.7.cloned.1.call-update) | async-done | bytes 1310736 | tf_op jit(solution)/shard_map/all_gather | solution.py:8
  42.3 1.0 slice.10
  43.3 3.5 %while.19 = (s32[]{:T(128)}, f32[2,32]{1,0:T(2,128)S(1)}, f32[2,32]{1,0:T(2,128)S(1)}, f32[2,32,1280]{2,1,0:T(8,128)S(1)}, f32[4,2,32]{2,1,0:T(2,128)S(1)}, /*in...) while((s32[]{:T(128)}, f32[2,32]{1,0:T(2,128)S(1)}, ...), condition=%wide.region_6.7_spmd, body=%wide.region_5.6_spmd.sunk | while | flops 246149 | bytes 985751 | solution.py:13
  43.3 1.1 fusion.121
  44.5 1.1 fusion.121
  45.6 1.1 fusion.121
  46.8 0.1 divide_convert_fusion
  46.9 0.2 copy.19
  47.0 11.4 %all_to_all.36 = bf16[2,32,1280]{2,0,1:T(2,128)(2,1)S(1)} all-to-all(bf16[2,32,1280]{2,0,1:T(2,128)(2,1)S(1)} %copy.19), channel_id=1, replica_groups=mesh['dp'=2,'tok'=4,'exp'=4] {'exp'}, dimensions={1} | all-to-all | bytes 327680 | tf_op jit(solution)/shard_map/all_to_all | solution.py:47
  58.4 0.1 copy.28
  58.5 0.1 all_to_all.29
  58.6 15.8 %convolution_bitcast_fusion = f32[8,8,1280]{2,0,1:T(8,128)S(1)} fusion(bf16[8,1024,1280]{2,1,0:T(8,128)(2,1)} %param.13, bf16[8,8,1280]{2,0,1:T(8,128)(2,1)S(1)} %all_to_all.29, bf16[8,1280,1024]{2,1,0:T(8,128)(2,1)} %param.12), kind=kOutput, calls=%fused_computation.12 | convolution fusion | flops 339804160 | bytes 42434560 | tf_op jit(solution)/shard_map/bef,efd->bed/dot_general | solution.py:52
  74.4 21.3 %all-reduce.1 = bf16[8,8,1280]{2,0,1:T(8,128)(2,1)S(1)} all-reduce(f32[8,8,1280]{2,0,1:T(8,128)S(1)} %convolution_bitcast_fusion), channel_id=1, replica_groups=mesh['dp'=2,'tok'=4,'exp'=4] {'tok'}, use_global_device_ids=true, to_apply=%region_7.8 | all-reduce | flops 81920 | bytes 491520 | tf_op jit(solution)/shard_map/psum | solution.py:53
  95.6 0.7 copy.21
  96.3 3.3 %all-to-all-start.1 = ((bf16[8,8,1280]{2,1,0:T(8,128)(2,1)}), bf16[8,8,1280]{2,1,0:T(8,128)(2,1)S(1)}, u32[]{:S(2)}, u32[]{:S(2)}) async-start(bf16[8,8,1280]{2,1,0:T(8,128)(2,1)} %copy.21), calls=%async_computation.1 | async-start | bytes 327680 | tf_op jit(solution)/shard_map/all_to_all | solution.py:54
  99.7 5.9 %all-to-all-done.1 = bf16[8,8,1280]{2,1,0:T(8,128)(2,1)S(1)} async-done(((bf16[8,8,1280]{2,1,0:T(8,128)(2,1)}), bf16[8,8,1280]{2,1,0:T(8,128)(2,1)S(1)}, u32[]{:S(2)}, u32[]{:S(2)}) %all-to-all-start.1) | async-done | bytes 163872 | tf_op jit(solution)/shard_map/all_to_all | solution.py:54
  105.7 1.6 %fusion.4 = bf16[2,256,1280]{2,1,0:T(8,128)(2,1)} fusion(pred[2,256]{1,0:T(4,128)(4,1)S(1)} %and_reduce_fusion, bf16[4,2,8,1280]{3,2,1,0:T(8,128)(2,1)S(1)} %bitcast.128, f32[2,256]{1,0:T(2,128)S(1)} %fusion.101, f32[2,256,32]{1,2,0:T(8,128)S(1)} %get-tuple-element.203), kind=kOutput, calls=%fused_computation.11 | convolution fusion | flops 43303456 | bytes 1542656 | tf_op jit(solution)/shard_map/bns,bsd->bnd/dot_general | solution.py:58
  (7 shorter events, 0.1 us)
Async XLA Ops:
  6.5 1.6 %copy-start = (bf16[2,256,1280]{2,1,0:T(8,128)(2,1)S(1)}, bf16[2,256,1280]{2,1,0:T(8,128)(2,1)}, u32[]{:S(2)}) copy-start(bf16[2,256,1280]{2,1,0:T(8,128)(2,1)} %param.8) | copy-start | bytes 3932164
  6.5 35.7 %all-gather.7.cloned.1.call-start = ((), (), s32[]{:S(2)}) async-start(), calls=%async_computation.2 | async-start | bytes 1638400 | tf_op jit(solution)/shard_map/all_gather | solution.py:8
  96.3 9.3 %all-to-all-start.1 = ((bf16[8,8,1280]{2,1,0:T(8,128)(2,1)}), bf16[8,8,1280]{2,1,0:T(8,128)(2,1)S(1)}, u32[]{:S(2)}, u32[]{:S(2)}) async-start(bf16[8,8,1280]{2,1,0:T(8,128)(2,1)} %copy.21), calls=%async_computation.1 | async-start | bytes 327680 | tf_op jit(solution)/shard_map/all_to_all | solution.py:54
Sparse Core Ops, SparseCore 0:
  10.8 31.3 all-gather.6
where the time goes:
time: 115 us; the launch traced here: 114 us
  blocking collectives  50.2 us (44%)
  matrix products  20 us (17%)
  waiting for transfers between devices  19.7 us (17%)
  between operations  13.5 us (12%)
  other arithmetic  5.26 us (5%)
  starting transfers between devices  3.35 us (3%)
  local copies, waits for them, and re-layouts  2.05 us (2%)
    psum x1, blocking collectives, shards(): summed = lax.psum(partial_out, 'tok')  21.3 us
    all_gather x2, blocking collectives, combined_all(): gathered = jax.tree.map(lambda a: lax.all_gather(a, axis), part)  17.6 us
    dot_general x1, matrix products, shards(): jnp.einsum('bef,efd->bed', hidden, expert_out, preferred_element_type=jnp...  15.8 us
    all_gather x1, waiting for transfers between devices, combined_all(): gathered = jax.tree.map(lambda a: lax.all_gather(a, axis), part)  13.8 us
    all_to_all x1, blocking collectives, shards(): lax.all_to_all(slot_in, 'exp', split_axis=1, concat_axis=0, tiled=True)  11.4 us
    all_to_all x1, waiting for transfers between devices, shards(): lax.all_to_all(summed.astype(jnp.bfloat16), 'exp', split_axis=0, concat_a...  5.93 us
    all_to_all x1, starting transfers between devices, shards(): lax.all_to_all(summed.astype(jnp.bfloat16), 'exp', split_axis=0, concat_a...  3.35 us
    add x3, other arithmetic, merge_parts(): earlier[2] * first_scale[..., None]  3.31 us
  transfers between devices with their start and end apart: 2, of which 2 were waited for; matrix products, arithmetic and copies ran while one was open for 0% of the time, Pallas kernels for 0%

commit v1 on v0

--- a/solution.py
+++ b/solution.py
@@ -50,7 +50,7 @@
         approximate=False,
     ).astype(jnp.bfloat16)
     partial_out = jnp.einsum("bef,efd->bed", hidden, expert_out, preferred_element_type=jnp.float32)
-    summed = lax.psum(partial_out, "tok")
+    summed = jnp.sum(lax.all_gather(partial_out, "tok"), axis=0)
     slot_out = lax.all_to_all(
         summed.astype(jnp.bfloat16), "exp", split_axis=0, concat_axis=1, tiled=True
     )

time: 115 us -> 124 us (1.078)
  waiting for transfers between devices: 19.7 us -> 46.7 us
  blocking collectives: 50.2 us -> 29 us
  other arithmetic: 5.26 us -> 6.66 us
  starting transfers between devices: 3.35 us -> 4.64 us
    all_gather x0 -> x1, waiting for transfers between devices: none -> 26.6 us  [shards(): summed = jnp.sum(lax.all_gather(partial_out, 'tok'), axis=0)]
    psum x1 -> x0, blocking collectives: 21.3 us -> none  [shards(): summed = lax.psum(partial_out, 'tok')]
    reduce_sum x0 -> x1, other arithmetic: none -> 1.4 us  [shards(): summed = jnp.sum(lax.all_gather(partial_out, 'tok'), axis=0)]
    all_to_all x1, starting transfers between devices: 3.35 us -> 4.6 us  [shards(): lax.all_to_all(summed.astype(jnp.bfloat16), 'exp', split_axis=0, concat_a...]
  transfers between devices with their start and end apart: 2 -> 3, of which waited for: 2 -> 3; matrix products, arithmetic and copies ran while one was open for 0% -> 0% of each run, Pallas kernels for 0% -> 0%
where the time goes in v1:
time: 124 us; the launch traced here: 123 us
  waiting for transfers between devices  46.7 us (38%)
  blocking collectives  29 us (23%)
  matrix products  20.8 us (17%)
  between operations  13.5 us (11%)
  other arithmetic  6.66 us (5%)
  starting transfers between devices  4.64 us (4%)
  local copies, waits for them, and re-layouts  2.05 us (2%)
    all_gather x1, waiting for transfers between devices, shards(): summed = jnp.sum(lax.all_gather(partial_out, 'tok'), axis=0)  26.6 us
    all_gather x2, blocking collectives, combined_all(): gathered = jax.tree.map(lambda a: lax.all_gather(a, axis), part)  17.6 us
    dot_general x1, matrix products, shards(): jnp.einsum('bef,efd->bed', hidden, expert_out, preferred_element_type=jnp...  16.6 us
    all_gather x1, waiting for transfers between devices, combined_all(): gathered = jax.tree.map(lambda a: lax.all_gather(a, axis), part)  13.7 us
    all_to_all x1, blocking collectives, shards(): lax.all_to_all(slot_in, 'exp', split_axis=1, concat_axis=0, tiled=True)  11.4 us
    all_to_all x1, waiting for transfers between devices, shards(): lax.all_to_all(summed.astype(jnp.bfloat16), 'exp', split_axis=0, concat_a...  6.38 us
    all_to_all x1, starting transfers between devices, shards(): lax.all_to_all(summed.astype(jnp.bfloat16), 'exp', split_axis=0, concat_a...  4.6 us
    add x3, other arithmetic, merge_parts(): earlier[2] * first_scale[..., None]  3.31 us
  transfers between devices with their start and end apart: 3, of which 3 were waited for; matrix products, arithmetic and copies ran while one was open for 0% of the time, Pallas kernels for 0%

profile of v1, /device:TPU:0, one launch (start us, length us, event | category | flops | bytes accessed | tf_op | source)
XLA Modules:
  0.0 123.4 jit_solution(3227964772109760489)
XLA Ops:
  6.5 0.0 copy-start
  6.5 0.0 all-gather.9.cloned.1.call-start
  6.5 0.8 add.75
  7.3 0.8 and_reduce_fusion
  8.1 0.0 copy-done
  8.1 1.5 %select_reduce_fusion = (f32[2,32]{1,0:T(2,128)S(1)}, f32[2,256,32]{1,2,0:T(8,128)S(1)}) fusion(pred[2,256]{1,0:T(4,128)(4,1)S(1)} %and_reduce_fusion, bf16[2,256,1280]{2,1,0:T(8,128)(2,1)S(1)} %copy-done, bf16[1280,32]{0,1:T(8,128)(2,1)} %param.9), kind=kOutput, calls=%fused_computation.77 | convolution fusion | flops 41975744 | bytes 1458944 | tf_op jit(solution)/shard_map/bnd,ds->bns/dot_general | solution.py:35
  9.6 1.1 fusion.62
  10.7 0.0 all-gather.9.cloned.1.call-update
  10.7 0.0 all-gather.11.cloned.1.call-start
  10.8 0.2 fusion.61
  10.9 9.6 %all-gather.5 = f32[4,2,32]{2,1,0:T(2,128)S(1)} all-gather(f32[1,2,32]{2,1,0:T(2,128)S(1)} %bitcast.132), channel_id=3, replica_groups=mesh['dp'=2,'tok'=4,'exp'=4] {'tok'}, dimensions={0}, use_global_device_ids=true | all-gather | bytes 1280 | tf_op jit(solution)/shard_map/all_gather | solution.py:8
  20.5 8.1 %all-gather.4 = f32[4,2,32]{2,1,0:T(2,128)S(1)} all-gather(f32[1,2,32]{2,1,0:T(2,128)S(1)} %bitcast.131), channel_id=2, replica_groups=mesh['dp'=2,'tok'=4,'exp'=4] {'tok'}, dimensions={0}, use_global_device_ids=true | all-gather | bytes 1280 | tf_op jit(solution)/shard_map/all_gather | solution.py:8
  28.6 13.7 %all-gather.9.cloned.1.call-done = f32[8,32,1280]{2,1,0:T(8,128)} async-done(((f32[2,32,1280]{2,1,0:T(8,128)}), f32[8,32,1280]{2,1,0:T(8,128)}) %all-gather.9.cloned.1.call-update) | async-done | bytes 1310736 | tf_op jit(solution)/shard_map/all_gather | solution.py:8
  42.3 1.0 slice.10
  43.3 3.5 %while.19 = (s32[]{:T(128)}, f32[2,32]{1,0:T(2,128)S(1)}, f32[2,32]{1,0:T(2,128)S(1)}, f32[2,32,1280]{2,1,0:T(8,128)S(1)}, f32[4,2,32]{2,1,0:T(2,128)S(1)}, /*in...) while((s32[]{:T(128)}, f32[2,32]{1,0:T(2,128)S(1)}, ...), condition=%wide.region_6.7_spmd, body=%wide.region_5.6_spmd.sunk | while | flops 246149 | bytes 985751 | solution.py:13
  43.3 1.1 fusion.121
  44.5 1.1 fusion.121
  45.6 1.1 fusion.121
  46.8 0.1 divide_convert_fusion
  46.9 0.2 copy.25
  47.0 11.4 %all_to_all.36 = bf16[2,32,1280]{2,0,1:T(2,128)(2,1)S(1)} all-to-all(bf16[2,32,1280]{2,0,1:T(2,128)(2,1)S(1)} %copy.25), channel_id=1, replica_groups=mesh['dp'=2,'tok'=4,'exp'=4] {'exp'}, dimensions={1} | all-to-all | bytes 327680 | tf_op jit(solution)/shard_map/all_to_all | solution.py:47
  58.4 0.1 copy.34
  58.5 0.1 all_to_all.29
  58.6 16.6 %convolution_bitcast_fusion = f32[8,8,1280]{2,0,1:T(8,128)} fusion(bf16[8,1024,1280]{2,1,0:T(8,128)(2,1)} %param.13, bf16[8,8,1280]{2,0,1:T(8,128)(2,1)S(1)} %all_to_all.29, bf16[8,1280,1024]{2,1,0:T(8,128)(2,1)} %param.12), kind=kOutput, calls=%fused_computation.12 | convolution fusion | flops 339804160 | bytes 42434560 | tf_op jit(solution)/shard_map/bef,efd->bed/dot_general | solution.py:52
  75.2 0.0 all-gather.11.cloned.1.call-update
  75.2 26.6 %all-gather.11.cloned.1.call-done = f32[32,8,1280]{2,0,1:T(8,128)} async-done(((f32[8,8,1280]{2,0,1:T(8,128)}), f32[32,8,1280]{2,0,1:T(8,128)}) %all-gather.11.cloned.1.call-update) | async-done | bytes 1310736 | tf_op jit(solution)/shard_map/all_gather | solution.py:53
  101.8 1.4 %bitcast_reduce_fusion = bf16[8,8,1280]{2,0,1:T(8,128)(2,1)S(1)} fusion(f32[32,8,1280]{2,0,1:T(8,128)} %all-gather.11.cloned.1.call-done), kind=kLoop, calls=%fused_computation.13 | loop fusion | flops 245760 | bytes 1474560 | tf_op jit(solution)/shard_map/reduce_sum | solution.py:53
  103.2 0.7 copy.27
  103.9 4.6 %all-to-all-start.1 = ((bf16[8,8,1280]{2,1,0:T(8,128)(2,1)}), bf16[8,8,1280]{2,1,0:T(8,128)(2,1)S(1)}, u32[]{:S(2)}, u32[]{:S(2)}) async-start(bf16[8,8,1280]{2,1,0:T(8,128)(2,1)} %copy.27), calls=%async_computation.1 | async-start | bytes 327680 | tf_op jit(solution)/shard_map/all_to_all | solution.py:54
  108.6 6.4 %all-to-all-done.1 = bf16[8,8,1280]{2,1,0:T(8,128)(2,1)S(1)} async-done(((bf16[8,8,1280]{2,1,0:T(8,128)(2,1)}), bf16[8,8,1280]{2,1,0:T(8,128)(2,1)S(1)}, u32[]{:S(2)}, u32[]{:S(2)}) %all-to-all-start.1) | async-done | bytes 163872 | tf_op jit(solution)/shard_map/all_to_all | solution.py:54
  115.0 1.6 %fusion.4 = bf16[2,256,1280]{2,1,0:T(8,128)(2,1)} fusion(pred[2,256]{1,0:T(4,128)(4,1)S(1)} %and_reduce_fusion, bf16[2,4,8,1280]{3,2,0,1:T(8,128)(2,1)S(1)} %bitcast.130, f32[2,256]{1,0:T(2,128)S(1)} %fusion.101, f32[2,256,32]{1,2,0:T(8,128)S(1)} %get-tuple-element.203), kind=kOutput, calls=%fused_computation.11 | convolution fusion | flops 43303456 | bytes 1542656 | tf_op jit(solution)/shard_map/bns,bsd->bnd/dot_general | solution.py:58
  (7 shorter events, 0.1 us)
Async XLA Ops:
  6.5 1.6 %copy-start = (bf16[2,256,1280]{2,1,0:T(8,128)(2,1)S(1)}, bf16[2,256,1280]{2,1,0:T(8,128)(2,1)}, u32[]{:S(2)}) copy-start(bf16[2,256,1280]{2,1,0:T(8,128)(2,1)} %param.8) | copy-start | bytes 3932164
  6.5 35.7 %all-gather.9.cloned.1.call-start = ((), (), s32[]{:S(2)}) async-start(), calls=%async_computation.2 | async-start | bytes 1638400 | tf_op jit(solution)/shard_map/all_gather | solution.py:8
  10.7 91.1 %all-gather.11.cloned.1.call-start = ((), (), s32[]{:S(2)}) async-start(), calls=%async_computation.3 | async-start | bytes 1638400 | tf_op jit(solution)/shard_map/all_gather | solution.py:53
  103.9 11.0 %all-to-all-start.1 = ((bf16[8,8,1280]{2,1,0:T(8,128)(2,1)}), bf16[8,8,1280]{2,1,0:T(8,128)(2,1)S(1)}, u32[]{:S(2)}, u32[]{:S(2)}) async-start(bf16[8,8,1280]{2,1,0:T(8,128)(2,1)} %copy.27), calls=%async_computation.1 | async-start | bytes 327680 | tf_op jit(solution)/shard_map/all_to_all | solution.py:54
Sparse Core Ops, SparseCore 0:
  10.8 31.3 all-gather.8
  75.4 26.4 all-gather.10
